TPU v7x, 32 devices: a whole 2x2x4 slice. The times are simulated.
32 devices in a mesh: grp: 4 (over y, x), shd: 8 (over z, core).
Axes of the slice: x: 2, y: 2, z: 4, core: 2. Of those that a mesh axis runs over, the one named last changes fastest.
Arguments:
- cells_in: bfloat16 [65536, 227], P(('grp', 'shd')), may hold values from -6 to 6
- targets: bfloat16 [65536, 227], P(('grp', 'shd')), may hold values from -6 to 6
- cell_areas: int32 [65536], P(('grp', 'shd')), may hold values from 1 to 32
- cell_node: int32 [65536], P(('grp', 'shd')), may hold values from 0 to 127, as said below
- adjacency: int32 [128, 8], P(('grp', 'shd')), may hold values from 0 to 15, as said below
- step_count: int32 [1], replicated, may hold values from 1 to 20
- weight_in: float32 [227, 512], P(None, 'shd'), may hold values from -0.375 to 0.375
- weight_layer: float32 [2, 512, 3072], P(None, 'shd'), may hold values from -2.1213203 to 2.1213203, as said below
- weight_dec: float32 [512, 739], P('shd'), may hold values from -0.25 to 0.25
- norm_gains: float32 [5, 512], P(None, 'shd'), may hold values from 0.2 to 4.8
- moment_in: float32 [227, 512], P(None, 'shd'), may hold values from -0.0007324219 to 0.0007324219
- moment_layer: float32 [2, 512, 3072], P(None, 'shd'), may hold values from -0.0007324219 to 0.0007324219
- moment_dec: float32 [512, 739], P('shd'), may hold values from -0.0007324219 to 0.0007324219
- moment_gains: float32 [5, 512], P(None, 'shd'), may hold values from -0.0007324219 to 0.0007324219
- square_in: float32 [227, 512], P(None, 'shd'), may hold values from 1.9215566e-08 to 1.9215565e-07
- square_layer: float32 [2, 512, 3072], P(None, 'shd'), may hold values from 1.9215566e-08 to 1.9215565e-07
- square_dec: float32 [512, 739], P('shd'), may hold values from 1.9215566e-08 to 1.9215565e-07
- square_gains: float32 [5, 512], P(None, 'shd'), may hold values from 1.9215566e-08 to 1.9215565e-07
Outputs:
- loss_value: float32 [], replicated
- grad_norm: float32 [], replicated
- delta_in: float32 [227, 512], P(None, 'shd')
- delta_layer: float32 [2, 512, 3072], P(None, 'shd')
- delta_dec: float32 [512, 739], P('shd')
- delta_gains: float32 [5, 512], P(None, 'shd')
- first_in: float32 [227, 512], P(None, 'shd')
- first_layer: float32 [2, 512, 3072], P(None, 'shd')
- first_dec: float32 [512, 739], P('shd')
- first_gains: float32 [5, 512], P(None, 'shd')
- second_in: float32 [227, 512], P(None, 'shd')
- second_layer: float32 [2, 512, 3072], P(None, 'shd')
- second_dec: float32 [512, 739], P('shd')
- second_gains: float32 [5, 512], P(None, 'shd')
Inputs may be any that keep to these rules, and one draw needn't show every extreme that they name: `cell_node`: within each aligned run of 512 cells every value occurs at least once; the run's cells belong to node block (run index) of the same device. `adjacency`: each row holds 8 distinct values. `weight_layer`: entries of the output block (columns 1536 up to 2048) lie within 8 times the bound of the other columns, which lie within 6 / sqrt(512).
All inputs are finite; a program needn't handle non-finite values.
Results may differ from a plain program's by a relative error of at most 0.028.
The roundings to bfloat16 on the way count: a program that leaves them out, or rounds other values in their place, can miss the bound.
Values may be sent and summed in bfloat16 or wider, within the bound.
No kernel may reach another device: no remote copies, remote signals or barrier semaphores. Data moves between devices by JAX's collectives and lax.ppermute only.
A program may use at most 256 MiB of HBM per device.

v0:
```python
import math

import jax
import jax.numpy as jnp
from jax import lax
from jax.sharding import PartitionSpec as P

D = 512
HEADS = 8
HEAD_DIM = 64
BLOCK = 128
SOURCES = 8
RATIO = 4
LAYERS = 2


eps_norm = 1e-05
score_scale = 0.125
clip_limit = 2.0
learn_rate = 0.02
decay_coef = 0.1
beta_one = 0.9
beta_two = 0.95
adam_eps = 1e-08


def product(left, right):
    return jnp.dot(left, right, preferred_element_type=jnp.float32)


def product_tn(left, right):
    return lax.dot_general(
        left, right, (((0,), (0,)), ((), ())), preferred_element_type=jnp.float32
    )


def product_nt(left, right):
    return lax.dot_general(
        left, right, (((1,), (1,)), ((), ())), preferred_element_type=jnp.float32
    )


def norm_parts(values):
    average = jnp.mean(values, axis=-1, keepdims=True)
    centered = values - average
    variance = jnp.mean(centered * centered, axis=-1, keepdims=True)
    inverse = lax.rsqrt(variance + eps_norm)
    return (centered * inverse, inverse)


def norm_back(grad_out, normal, inverse, gain_row):
    grad_normal = grad_out * gain_row
    grad_gain = jnp.sum(grad_out * normal, axis=0)
    mean_first = jnp.mean(grad_normal, axis=-1, keepdims=True)
    mean_second = jnp.mean(grad_normal * normal, axis=-1, keepdims=True)
    return (inverse * (grad_normal - mean_first - normal * mean_second), grad_gain)


def silu_grad(values):
    sigma = jax.nn.sigmoid(values)
    return sigma * (1.0 + values * (1.0 - sigma))


def attend_forward(query_grp, key_grp, value_grp):
    scores = (
        jnp.einsum("gqhd,gkhd->ghqk", query_grp, key_grp, preferred_element_type=jnp.float32)
        * score_scale
    )
    largest = jnp.max(scores, axis=-1, keepdims=True)
    exponent = jnp.exp(scores - largest)
    denominator = jnp.sum(exponent, axis=-1, keepdims=True)
    probs = exponent / denominator
    output = jnp.einsum(
        "ghqk,gkhd->gqhd", probs.astype(jnp.bfloat16), value_grp, preferred_element_type=jnp.float32
    )
    return (output.astype(jnp.bfloat16), largest + jnp.log(denominator))


def attend_backward(query_grp, key_grp, value_grp, log_sum, grad_out):
    scores = (
        jnp.einsum("gqhd,gkhd->ghqk", query_grp, key_grp, preferred_element_type=jnp.float32)
        * score_scale
    )
    probs = jnp.exp(scores - log_sum)
    grad_probs = jnp.einsum(
        "gqhd,gkhd->ghqk", grad_out, value_grp, preferred_element_type=jnp.float32
    )
    inner_sum = jnp.sum(probs * grad_probs, axis=-1, keepdims=True)
    grad_scores = (probs * (grad_probs - inner_sum)).astype(jnp.bfloat16)
    grad_query = (
        jnp.einsum("ghqk,gkhd->gqhd", grad_scores, key_grp, preferred_element_type=jnp.float32)
        * score_scale
    )
    grad_key = (
        jnp.einsum("ghqk,gqhd->gkhd", grad_scores, query_grp, preferred_element_type=jnp.float32)
        * score_scale
    )
    grad_value = jnp.einsum(
        "ghqk,gqhd->gkhd", probs.astype(jnp.bfloat16), grad_out, preferred_element_type=jnp.float32
    )
    return (grad_query, grad_key, grad_value)


def attend_all(queries, source_pool, adjacency):
    local_blocks = adjacency.shape[0]
    group_size = math.gcd(4, local_blocks)
    pool_view = source_pool.reshape(-1, BLOCK, 2 * D)
    query_groups = queries.reshape(local_blocks // group_size, group_size, BLOCK, HEADS, HEAD_DIM)
    index_groups = adjacency.reshape(local_blocks // group_size, group_size, SOURCES)

    def one_group(group_items):
        query_grp, indices = group_items
        picked = pool_view[indices].reshape(group_size, SOURCES * BLOCK, 2, HEADS, HEAD_DIM)
        return attend_forward(query_grp, picked[:, :, 0], picked[:, :, 1])

    outputs, log_sums = lax.map(one_group, (query_groups, index_groups))
    return (outputs.reshape(local_blocks * BLOCK, D), log_sums)


def attend_back_all(queries, source_pool, adjacency, log_sums, grad_attended):
    local_blocks = adjacency.shape[0]
    group_size = math.gcd(4, local_blocks)
    pool_view = source_pool.reshape(-1, BLOCK, 2 * D)
    query_groups = queries.reshape(local_blocks // group_size, group_size, BLOCK, HEADS, HEAD_DIM)
    grad_groups = grad_attended.reshape(
        local_blocks // group_size, group_size, BLOCK, HEADS, HEAD_DIM
    )
    index_groups = adjacency.reshape(local_blocks // group_size, group_size, SOURCES)

    def one_group(carried, group_items):
        query_grp, indices, log_sum, grad_grp = group_items
        picked = pool_view[indices].reshape(group_size, SOURCES * BLOCK, 2, HEADS, HEAD_DIM)
        grad_query, grad_key, grad_value = attend_backward(
            query_grp, picked[:, :, 0], picked[:, :, 1], log_sum, grad_grp
        )
        stacked = jnp.stack([grad_key, grad_value], axis=2).reshape(
            group_size * SOURCES, BLOCK, 2 * D
        )
        carried = carried.at[indices.reshape(-1)].add(stacked)
        return (carried, grad_query)

    initial = jnp.zeros((pool_view.shape[0], BLOCK, 2 * D), jnp.float32)
    grad_pool, grad_queries = lax.scan(
        one_group, initial, (query_groups, index_groups, log_sums, grad_groups)
    )
    return (grad_queries.reshape(local_blocks * BLOCK, D), grad_pool.reshape(-1, 2 * D))


def adam_step(gradient, weight, moment, square, factor, first_fix, second_fix, weight_decay):
    clipped = gradient * factor
    first = beta_one * moment + (1.0 - beta_one) * clipped
    second = beta_two * square + (1.0 - beta_two) * clipped * clipped
    delta = -learn_rate * (
        first / first_fix / (jnp.sqrt(second / second_fix) + adam_eps) + weight_decay * weight
    )
    return (delta, first, second)


def local(
    cells_in,
    targets,
    cell_areas,
    cell_node,
    adjacency,
    step_count,
    weight_in,
    weight_layer,
    weight_dec,
    norm_gains,
    moment_in,
    moment_layer,
    moment_dec,
    moment_gains,
    square_in,
    square_layer,
    square_dec,
    square_gains,
):
    grid_rows = cells_in.shape[0]
    node_rows = grid_rows // RATIO
    local_blocks = node_rows // BLOCK
    cell_block = RATIO * BLOCK
    areas_f = cell_areas.astype(jnp.float32)
    area_total = lax.psum(jnp.sum(areas_f), ("grp", "shd"))
    low_in, low_layer, low_dec, low_gains = (
        lax.all_gather(weight_in.astype(jnp.bfloat16), "shd", axis=1, tiled=True),
        lax.all_gather(weight_layer.astype(jnp.bfloat16), "shd", axis=1, tiled=True),
        lax.all_gather(weight_dec.astype(jnp.bfloat16), "shd", axis=0, tiled=True),
        lax.all_gather(norm_gains.astype(jnp.bfloat16), "shd", axis=1, tiled=True),
    )
    gain_all = low_gains.astype(jnp.float32)
    encoded = product(cells_in, low_in).astype(jnp.bfloat16)
    onehot = (
        cell_node.reshape(local_blocks, cell_block)[:, :, None]
        == jnp.arange(BLOCK, dtype=jnp.int32)[None, None, :]
    ).astype(jnp.bfloat16)
    summed = jnp.einsum(
        "bcn,bcd->bnd",
        onehot,
        encoded.reshape(local_blocks, cell_block, D),
        preferred_element_type=jnp.float32,
    )
    counts = jnp.sum(onehot.astype(jnp.float32), axis=1)
    hidden = (summed / counts[:, :, None]).reshape(node_rows, D)
    kept_values = []
    for layer_idx in range(LAYERS):
        matrices = low_layer[layer_idx]
        normal_one, inverse_one = norm_parts(hidden)
        normed_one = (normal_one * gain_all[2 * layer_idx]).astype(jnp.bfloat16)
        projected = product(normed_one, matrices[:, : 3 * D]).astype(jnp.bfloat16)
        source_pool = lax.all_gather(projected[:, D:], "grp", axis=0, tiled=True)
        attended, log_sums = attend_all(projected[:, :D], source_pool, adjacency)
        middle = hidden + product(attended, matrices[:, 3 * D : 4 * D])
        normal_two, inverse_two = norm_parts(middle)
        normed_two = (normal_two * gain_all[2 * layer_idx + 1]).astype(jnp.bfloat16)
        inner_up = product(normed_two, matrices[:, 4 * D : 5 * D])
        activated = jax.nn.silu(inner_up).astype(jnp.bfloat16)
        hidden = middle + product(activated, matrices[:, 5 * D :])
        kept_pool = source_pool
        kept_values.append(
            (
                normal_one,
                inverse_one,
                normed_one,
                projected,
                kept_pool,
                attended,
                log_sums,
                normal_two,
                inverse_two,
                normed_two,
                inner_up,
                activated,
            )
        )
    node_low = hidden.astype(jnp.bfloat16).reshape(local_blocks, BLOCK, D)
    spread = jnp.einsum(
        "bcn,bnd->bcd", onehot, node_low, preferred_element_type=jnp.float32
    ).reshape(grid_rows, D)
    combined = encoded.astype(jnp.float32) + spread
    normal_dec, inverse_dec = norm_parts(combined)
    normed_dec = (normal_dec * gain_all[2 * LAYERS]).astype(jnp.bfloat16)
    inner_dec = product(normed_dec, low_dec[:, :D])
    activated_dec = jax.nn.silu(inner_dec).astype(jnp.bfloat16)
    predicted = product(activated_dec, low_dec[:, D:])
    errors = predicted - targets.astype(jnp.float32)
    weighted = areas_f[:, None] * errors
    loss_part = jnp.sum(weighted * errors) / area_total
    grad_pred = (2.0 * weighted / area_total).astype(jnp.bfloat16)
    grad_dec_out = product_tn(activated_dec, grad_pred)
    grad_act_dec = product_nt(grad_pred, low_dec[:, D:])
    grad_inner_dec = (grad_act_dec * silu_grad(inner_dec)).astype(jnp.bfloat16)
    grad_dec_in = product_tn(normed_dec, grad_inner_dec)
    grad_normed_dec = product_nt(grad_inner_dec, low_dec[:, :D])
    grad_combined_f, grad_gain_dec = norm_back(
        grad_normed_dec, normal_dec, inverse_dec, gain_all[2 * LAYERS]
    )
    grad_combined = grad_combined_f.astype(jnp.bfloat16)
    grad_hidden = jnp.einsum(
        "bcn,bcd->bnd",
        onehot,
        grad_combined.reshape(local_blocks, cell_block, D),
        preferred_element_type=jnp.float32,
    ).reshape(node_rows, D)
    gain_grads = [None] * (2 * LAYERS + 1)
    gain_grads[2 * LAYERS] = grad_gain_dec
    layer_grads = [None] * LAYERS
    for layer_idx in reversed(range(LAYERS)):
        (
            normal_one,
            inverse_one,
            normed_one,
            projected,
            kept_pool,
            attended,
            log_sums,
            normal_two,
            inverse_two,
            normed_two,
            inner_up,
            activated,
        ) = kept_values[layer_idx]
        matrices = low_layer[layer_idx]
        grad_out_low = grad_hidden.astype(jnp.bfloat16)
        grad_down = product_tn(activated, grad_out_low)
        grad_act = product_nt(grad_out_low, matrices[:, 5 * D :])
        grad_inner = (grad_act * silu_grad(inner_up)).astype(jnp.bfloat16)
        grad_up = product_tn(normed_two, grad_inner)
        grad_normed_two = product_nt(grad_inner, matrices[:, 4 * D : 5 * D])
        grad_mid_norm, gain_grads[2 * layer_idx + 1] = norm_back(
            grad_normed_two, normal_two, inverse_two, gain_all[2 * layer_idx + 1]
        )
        grad_middle = grad_hidden + grad_mid_norm
        grad_branch = grad_middle.astype(jnp.bfloat16)
        grad_out_proj = product_tn(attended, grad_branch)
        grad_attended = product_nt(grad_branch, matrices[:, 3 * D : 4 * D]).astype(jnp.bfloat16)
        source_pool = kept_pool
        grad_queries, grad_pool = attend_back_all(
            projected[:, :D], source_pool, adjacency, log_sums, grad_attended
        )
        grad_kv = lax.psum_scatter(
            grad_pool.astype(jnp.bfloat16), "grp", scatter_dimension=0, tiled=True
        ).astype(jnp.float32)
        grad_proj = jnp.concatenate([grad_queries, grad_kv], axis=1).astype(jnp.bfloat16)
        grad_qkv_w = product_tn(normed_one, grad_proj)
        grad_normed_one = product_nt(grad_proj, matrices[:, : 3 * D])
        grad_first, gain_grads[2 * layer_idx] = norm_back(
            grad_normed_one, normal_one, inverse_one, gain_all[2 * layer_idx]
        )
        grad_hidden = grad_middle + grad_first
        layer_grads[layer_idx] = jnp.concatenate(
            [grad_qkv_w, grad_out_proj, grad_up, grad_down], axis=1
        )
    grad_summed = (grad_hidden.reshape(local_blocks, BLOCK, D) / counts[:, :, None]).astype(
        jnp.bfloat16
    )
    grad_from_nodes = jnp.einsum(
        "bcn,bnd->bcd", onehot, grad_summed, preferred_element_type=jnp.float32
    ).reshape(grid_rows, D)
    grad_encoded = (grad_combined.astype(jnp.float32) + grad_from_nodes).astype(jnp.bfloat16)
    grad_in = product_tn(cells_in, grad_encoded)
    grad_layer = jnp.stack(layer_grads, axis=0)
    grad_dec = jnp.concatenate([grad_dec_in, grad_dec_out], axis=1)
    grad_gains = jnp.stack(gain_grads, axis=0)
    full_sums = (
        lax.psum(grad_in.astype(jnp.bfloat16), "grp").astype(jnp.float32),
        lax.psum(grad_layer.astype(jnp.bfloat16), "grp").astype(jnp.float32),
        lax.psum(grad_dec.astype(jnp.bfloat16), "grp").astype(jnp.float32),
        lax.psum(grad_gains.astype(jnp.bfloat16), "grp").astype(jnp.float32),
        lax.psum(loss_part.astype(jnp.bfloat16), "grp").astype(jnp.float32),
    )
    shard_grads = (
        lax.psum_scatter(
            full_sums[0].astype(jnp.bfloat16), "shd", scatter_dimension=1, tiled=True
        ).astype(jnp.float32),
        lax.psum_scatter(
            full_sums[1].astype(jnp.bfloat16), "shd", scatter_dimension=1, tiled=True
        ).astype(jnp.float32),
        lax.psum_scatter(
            full_sums[2].astype(jnp.bfloat16), "shd", scatter_dimension=0, tiled=True
        ).astype(jnp.float32),
        lax.psum_scatter(
            full_sums[3].astype(jnp.bfloat16), "shd", scatter_dimension=1, tiled=True
        ).astype(jnp.float32),
    )
    group_sums = (shard_grads[0], shard_grads[1], shard_grads[2], shard_grads[3], full_sums[4])
    squares_part = jnp.float32(0.0)
    for index_w in range(4):
        squares_part = squares_part + jnp.sum(group_sums[index_w] * group_sums[index_w])
    total_squares, loss_value = lax.psum((squares_part, group_sums[4]), "shd")
    grad_norm = jnp.sqrt(total_squares)
    factor = clip_limit / jnp.maximum(grad_norm, clip_limit)
    step_value = step_count[0].astype(jnp.float32)
    first_fix = 1.0 - jnp.power(jnp.float32(beta_one), step_value)
    second_fix = 1.0 - jnp.power(jnp.float32(beta_two), step_value)
    weights = (weight_in, weight_layer, weight_dec, norm_gains)
    moments = (moment_in, moment_layer, moment_dec, moment_gains)
    squared = (square_in, square_layer, square_dec, square_gains)
    decays = (decay_coef, decay_coef, decay_coef, 0.0)
    deltas, firsts, seconds = ([], [], [])
    for index_w in range(4):
        delta, first, second = adam_step(
            group_sums[index_w],
            weights[index_w],
            moments[index_w],
            squared[index_w],
            factor,
            first_fix,
            second_fix,
            decays[index_w],
        )
        deltas.append(delta)
        firsts.append(first)
        seconds.append(second)
    return (
        loss_value,
        grad_norm,
        deltas[0],
        deltas[1],
        deltas[2],
        deltas[3],
        firsts[0],
        firsts[1],
        firsts[2],
        firsts[3],
        seconds[0],
        seconds[1],
        seconds[2],
        seconds[3],
    )


def solution(mesh):
    return jax.shard_map(
        local,
        mesh=mesh,
        in_specs=(
            P(("grp", "shd"), None),
            P(("grp", "shd"), None),
            P(("grp", "shd")),
            P(("grp", "shd")),
            P(("grp", "shd"), None),
            P(),
            P(None, "shd"),
            P(None, "shd", None),
            P("shd", None),
            P(None, "shd"),
            P(None, "shd"),
            P(None, "shd", None),
            P("shd", None),
            P(None, "shd"),
            P(None, "shd"),
            P(None, "shd", None),
            P("shd", None),
            P(None, "shd"),
        ),
        out_specs=(
            P(),
            P(),
            P(None, "shd"),
            P(None, "shd", None),
            P("shd", None),
            P(None, "shd"),
            P(None, "shd"),
            P(None, "shd", None),
            P("shd", None),
            P(None, "shd"),
            P(None, "shd"),
            P(None, "shd", None),
            P("shd", None),
            P(None, "shd"),
        ),
        check_vma=False,
    )
```

profile of v0, /device:TPU:0, one launch (start us, length us, event | category | flops | bytes accessed | tf_op | source)
XLA Modules:
  0.0 1075.0 jit_solution(6061040492452267748)
XLA Ops:
  12.0 14.6 %all-gather = bf16[8,64,5]{1,2,0:T(8,128)(2,1)S(1)} all-gather(bf16[1,64,5]{1,2,0:T(8,128)(2,1)S(1)} %convert_bitcast_fusion), channel_id=1, replica_groups=mesh['grp'=4,'shd'=8] {'shd'}, dimensions={0}, use_global_device_ids=true | all-gather | bytes 5760 | tf_op jit(solution)/shard_map/all_gather | solution.py:189
  26.7 15.4 %all_gather.18 = bf16[227,512]{0,1:T(8,128)(2,1)S(1)} all-gather(bf16[227,64]{0,1:T(8,128)(2,1)S(1)} %convert_element_type.202), channel_id=1, replica_groups=mesh['grp'=4,'shd'=8] {'shd'}, dimensions={1}, use_global_device_ids=true | all-gather | bytes 261504 | tf_op jit(solution)/shard_map/all_gather | solution.py:186
  47.0 32.7 %all-gather.5.cloned.1.call-done = bf16[2,512,3072]{2,1,0:T(8,128)(2,1)} async-done(((bf16[2,64,3072]{2,1,0:T(8,128)(2,1)}), bf16[2,512,3072]{2,1,0:T(8,128)(2,1)}) %all-gather.5.cloned.1.call-update) | async-done | bytes 6291472 | tf_op jit(solution)/shard_map/all_gather | solution.py:187
  94.1 46.9 %all-gather.7.cloned.1.call-done = bf16[2048,1024]{1,0:T(8,128)(2,1)} async-done(((bf16[512,1024]{1,0:T(8,128)(2,1)}), bf16[2048,1024]{1,0:T(8,128)(2,1)}) %all-gather.7.cloned.1.call-update) | async-done | bytes 4194320 | tf_op jit(solution)/shard_map/all_gather | solution.py:211
  148.6 22.1 %reshape.380 = bf16[4,1024,2,8,64]{4,3,2,1,0:T(8,128)(2,1)} reshape(bf16[32,128,1024]{2,1,0:T(8,128)(2,1)} %gather_fusion) | data formatting | bytes 16777216 | tf_op jit(solution)/shard_map/while/body/eval_jaxpr/reshape | solution.py:113
  227.6 40.5 %psum.56 = f32[]{:T(128)} all-reduce(f32[]{:T(128)} %convert_reduce_fusion.1), channel_id=1, replica_groups=mesh['grp'=4,'shd'=8] {'grp','shd'}, use_global_device_ids=true, to_apply=%region_17.18 | all-reduce | flops 1 | bytes 8 | tf_op jit(solution)/shard_map/psum | solution.py:184
  268.7 16.5 %all_gather.23 = bf16[512,739]{1,0:T(8,128)(2,1)} all-gather(bf16[64,739]{1,0:T(8,128)(2,1)S(1)} %convert_element_type.226), channel_id=1, replica_groups=mesh['grp'=4,'shd'=8] {'shd'}, dimensions={0}, use_global_device_ids=true | all-gather | bytes 851328 | tf_op jit(solution)/shard_map/all_gather | solution.py:188
  297.0 22.1 %reshape.382 = bf16[4,1024,2,8,64]{4,3,2,1,0:T(8,128)(2,1)} reshape(bf16[32,128,1024]{2,1,0:T(8,128)(2,1)} %gather_fusion.1) | data formatting | bytes 16777216 | tf_op jit(solution)/shard_map/while/body/eval_jaxpr/reshape | solution.py:113
  394.4 13.1 %multiply_reduce_fusion.1 = (f32[4,8,128]{2,1,0:T(8,128)S(1)}, f32[4,8,128,1024]{3,2,1,0:T(8,128)}) fusion(f32[4,8,128,1024]{3,2,1,0:T(8,128)} %copy-done.2, f32[4,8,128]{2,1,0:T(8,128)S(1)} %log_add_fusion.1, bf16[4,128,8,64]{1,3,2,0:T(8,128)(2,1)S(1)} %copy.219, bf16[4,1024,1,8,64]{1,4,3,0,2:T(8,128)(2,1)} %copy.278), kind=kOutput, calls=%fused_computation.10 | convolution fusion | flops 553644032 | bytes 38305792 | tf_op jit(solution)/shard_map/while/body/eval_jaxpr/gqhd,gkhd->ghqk/dot_general | solution.py:85
  441.8 27.5 %copy.251 = f32[4,1024,2,8,64]{4,3,2,1,0:T(8,128)} copy(f32[4,1024,2,8,64]{1,4,3,0,2:T(8,128)} %pad_maximum_fusion) | data formatting | bytes 33554432 | tf_op jit(solution)/shard_map/while/body/eval_jaxpr/reshape | solution.py:136
  469.3 28.3 %reshape.371 = f32[32,128,1024]{2,1,0:T(8,128)} reshape(f32[4,1024,2,8,64]{4,3,2,1,0:T(8,128)} %copy.251) | data formatting | bytes 33554432 | tf_op jit(solution)/shard_map/while/body/eval_jaxpr/reshape | solution.py:136
  501.9 35.9 %scatter_fusion = f32[16,128,1024]{2,1,0:T(8,128)} fusion(f32[16,128,1024]{2,1,0:T(8,128)} %broadcast.279.clone, s32[32]{0:T(128)S(1)} %copy-done.111, f32[32,128,1024]{2,1,0:T(8,128)} %reshape.371), kind=kCustom, calls=%fused_computation.2 | custom fusion | flops 4194304 | bytes 50331776 | tf_op jit(solution)/shard_map/while/body/eval_jaxpr/scatter-add | solution.py:139
  556.7 41.3 %reduce-scatter.13.cloned.1.call-done = bf16[512,1024]{1,0:T(8,128)(2,1)} async-done(((bf16[2048,1024]{1,0:T(8,128)(2,1)}), bf16[512,1024]{1,0:T(8,128)(2,1)}) %reduce-scatter.13.cloned.1.call-update) | async-done | bytes 1048592 | tf_op jit(solution)/shard_map/reduce_scatter | solution.py:301
  612.0 12.7 %multiply_reduce_fusion = (f32[4,8,128]{2,1,0:T(8,128)S(1)}, f32[4,8,128,1024]{3,2,1,0:T(8,128)}) fusion(f32[4,8,128,1024]{3,2,1,0:T(8,128)} %copy-done.1, f32[4,8,128]{2,1,0:T(8,128)S(1)} %log_add_fusion, bf16[4,128,8,64]{1,3,2,0:T(8,128)(2,1)S(1)} %copy.227, bf16[4,1024,1,8,64]{1,4,3,0,2:T(8,128)(2,1)} %copy.276), kind=kOutput, calls=%fused_computation.7 | convolution fusion | flops 553644032 | bytes 38305792 | tf_op jit(solution)/shard_map/while/body/eval_jaxpr/gqhd,gkhd->ghqk/dot_general | solution.py:85
  658.9 27.7 %copy.253 = f32[4,1024,2,8,64]{4,3,2,1,0:T(8,128)} copy(f32[4,1024,2,8,64]{1,4,3,0,2:T(8,128)} %pad_maximum_fusion.1) | data formatting | bytes 33554432 | tf_op jit(solution)/shard_map/while/body/eval_jaxpr/reshape | solution.py:136
  686.7 28.3 %reshape.373 = f32[32,128,1024]{2,1,0:T(8,128)} reshape(f32[4,1024,2,8,64]{4,3,2,1,0:T(8,128)} %copy.253) | data formatting | bytes 33554432 | tf_op jit(solution)/shard_map/while/body/eval_jaxpr/reshape | solution.py:136
  719.3 35.9 %scatter_fusion.1 = f32[16,128,1024]{2,1,0:T(8,128)} fusion(f32[16,128,1024]{2,1,0:T(8,128)} %broadcast.279, s32[32]{0:T(128)S(1)} %copy-done.111, f32[32,128,1024]{2,1,0:T(8,128)} %reshape.373), kind=kCustom, calls=%fused_computation.3 | custom fusion | flops 4194304 | bytes 50331776 | tf_op jit(solution)/shard_map/while/body/eval_jaxpr/scatter-add | solution.py:139
  798.8 15.4 %reduce-scatter.15.cloned.1.call-done = bf16[512,1024]{1,0:T(8,128)(2,1)} async-done(((bf16[2048,1024]{1,0:T(8,128)(2,1)}), bf16[512,1024]{1,0:T(8,128)(2,1)}) %reduce-scatter.15.cloned.1.call-update) | async-done | bytes 1048592 | tf_op jit(solution)/shard_map/reduce_scatter | solution.py:301
  848.3 70.3 %reduce-scatter.17.cloned.1.call-done = bf16[2,64,3072]{2,1,0:T(8,128)(2,1)} async-done(((bf16[2,512,3072]{2,1,0:T(8,128)(2,1)}), bf16[2,64,3072]{2,1,0:T(8,128)(2,1)}) %reduce-scatter.17.cloned.1.call-update) | async-done | bytes 786448 | tf_op jit(solution)/shard_map/reduce_scatter | solution.py:336
  920.7 29.8 %reduce-scatter.23.cloned.1.call-done = bf16[64,5]{1,0:T(8,128)(2,1)} async-done(((bf16[512,5]{1,0:T(8,128)(2,1)}), bf16[64,5]{1,0:T(8,128)(2,1)}) %reduce-scatter.23.cloned.1.call-update) | async-done | bytes 656
  951.3 31.0 %reduce-scatter.19.cloned.1.call-done = bf16[64,227]{1,0:T(8,128)(2,1)} async-done(((bf16[512,227]{1,0:T(8,128)(2,1)}), bf16[64,227]{1,0:T(8,128)(2,1)}) %reduce-scatter.19.cloned.1.call-update) | async-done | bytes 29072
  982.3 17.8 %all-reduce.1 = (bf16[]{:T(256)}, bf16[227,64]{0,1:T(8,128)(2,1)S(1)}, bf16[5,64]{1,0:T(8,128)(2,1)S(1)}) all-reduce(bf16[]{:T(256)S(6)} %div.198, bf16[227,64]{0,1:T(8,128)(2,1)} %bitcast.220, bf16[5,64]{1,0:T(8,128)(2,1)S(1)} %copy.259), channel_id=1, replica_groups=mesh['grp'=4,'shd'=8] {'grp'}, use_global_device_ids=true, to_apply=%region_18.19 | all-reduce | flops 14849 | bytes 59396 | tf_op jit(solution)/shard_map/psum | solution.py:330
  1001.3 32.9 %all-reduce.5.cloned.1.call-done = (bf16[2,64,3072]{2,1,0:T(8,128)(2,1)}, bf16[64,739]{1,0:T(8,128)(2,1)}) async-done(((bf16[2,64,3072]{2,1,0:T(8,128)(2,1)}, bf16[64,739]{1,0:T(8,128)(2,1)}), (bf16[2,64,3072]{2,1,0:T(8,128)(2,1)}, bf16[64,739]{1,0:T(8,128)(2,1)})) %all-reduce.5.cloned.1.call-update) | async-done | bytes 881040 | tf_op jit(solution)/shard_map/psum | solution.py:327
  1040.5 17.1 %all-reduce = (f32[]{:T(128)}, f32[]{:T(128)}) all-reduce(bf16[]{:T(256)} %get-tuple-element.171, f32[]{:T(128)S(6)} %add.275), channel_id=1, replica_groups=mesh['grp'=4,'shd'=8] {'shd'}, use_global_device_ids=true, to_apply=%region_19.20 | all-reduce | flops 2 | bytes 14 | tf_op jit(solution)/shard_map/psum | solution.py:350
  (417 shorter events, 376.5 us)
Async XLA Ops:
  7.2 72.5 %all-gather.5.cloned.1.call-start = ((), (), s32[]{:S(2)}) async-start(), calls=%async_computation.6 | async-start | bytes 7077888 | tf_op jit(solution)/shard_map/all_gather | solution.py:187
  9.7 131.2 %all-gather.7.cloned.1.call-start = ((), (), s32[]{:S(2)}) async-start(), calls=%async_computation.7 | async-start | bytes 5242880 | tf_op jit(solution)/shard_map/all_gather | solution.py:211
  10.5 375.7 %copy-start.67 = (s32[4,512]{1,0:T(4,128)}, s32[4,512]{1,0:T(4,128)S(1)}, u32[]{:S(2)}) copy-start(s32[4,512]{1,0:T(4,128)S(1)} %eq.15) | copy-start | bytes 24580
  46.4 172.5 %copy-start.11 = (f32[4,128,512]{2,1,0:T(8,128)}, f32[4,128,512]{2,1,0:T(8,128)S(1)}, u32[]{:S(2)}) copy-start(f32[4,128,512]{2,1,0:T(8,128)S(1)} %get-tuple-element.204) | copy-start | bytes 3145732
  46.7 173.1 %copy-start.93 = (f32[1,512]{1,0:T(1,128)}, f32[1,512]{1,0:T(1,128)S(1)}, u32[]{:S(2)}) copy-start(f32[1,512]{1,0:T(1,128)S(1)} %get-tuple-element.199) | copy-start | bytes 6148
  46.7 175.2 %copy-start.104 = (f32[1,512]{1,0:T(1,128)}, f32[1,512]{1,0:T(1,128)S(1)}, u32[]{:S(2)}) copy-start(f32[1,512]{1,0:T(1,128)S(1)} %get-tuple-element.198) | copy-start | bytes 6148
  46.7 343.5 %copy-start.95 = (f32[1,512]{1,0:T(1,128)}, f32[1,512]{1,0:T(1,128)S(1)}, u32[]{:S(2)}) copy-start(f32[1,512]{1,0:T(1,128)S(1)} %get-tuple-element.197) | copy-start | bytes 6148
  89.6 200.0 %all-gather.9.cloned.1.call-start = ((), (), s32[]{:S(2)}) async-start(), calls=%async_computation.8 | async-start | bytes 5242880 | tf_op jit(solution)/shard_map/all_gather | solution.py:211
  221.5 145.2 %copy-start.21 = (f32[512,512]{1,0:T(8,128)}, f32[512,512]{1,0:T(8,128)S(1)}, u32[]{:S(2)}) copy-start(f32[512,512]{1,0:T(8,128)S(1)} %get-tuple-element.210) | copy-start | bytes 3145732
  226.9 371.1 %reduce-scatter.13.cloned.1.call-start = ((), (), s32[]{:S(2)}) async-start(), calls=%async_computation.9 | async-start | bytes 5242880 | tf_op jit(solution)/shard_map/reduce_scatter | solution.py:301
  390.6 213.4 %copy-start.18 = (f32[512,512]{1,0:T(8,128)}, f32[512,512]{1,0:T(8,128)S(1)}, u32[]{:S(2)}) copy-start(f32[512,512]{1,0:T(8,128)S(1)} %bitcast_add_fusion.2) | copy-start | bytes 3145732
  544.0 270.2 %reduce-scatter.15.cloned.1.call-start = ((), (), s32[]{:S(2)}) async-start(), calls=%async_computation.10 | async-start | bytes 5242880 | tf_op jit(solution)/shard_map/reduce_scatter | solution.py:301
  761.3 87.0 %reduce-scatter.21.cloned.1.call-start = ((), (), s32[]{:S(2)}) async-start(), calls=%async_computation.13 | async-start | bytes 884736 | tf_op jit(solution)/shard_map/reduce_scatter | solution.py:339
  775.9 142.7 %reduce-scatter.17.cloned.1.call-start = ((), (), s32[]{:S(2)}) async-start(), calls=%async_computation.11 | async-start | bytes 7077888 | tf_op jit(solution)/shard_map/reduce_scatter | solution.py:336
  824.3 126.2 %reduce-scatter.23.cloned.1.call-start = ((), (), s32[]{:S(2)}) async-start(), calls=%async_computation.14 | async-start | bytes 147456
  835.8 222.5 %copy-start.101 = (f32[5,64]{1,0:T(8,128)S(1)}, f32[5,64]{1,0:T(8,128)}, u32[]{:S(2)}) copy-start(f32[5,64]{1,0:T(8,128)} %param.27) | copy-start | bytes 3844
  835.8 222.5 %copy-start.109 = (f32[5,64]{1,0:T(8,128)S(1)}, f32[5,64]{1,0:T(8,128)}, u32[]{:S(2)}) copy-start(f32[5,64]{1,0:T(8,128)} %param.35) | copy-start | bytes 3844
  835.8 222.5 %copy-start.110 = (f32[5,64]{1,0:T(8,128)S(1)}, f32[5,64]{1,0:T(8,128)}, u32[]{:S(2)}) copy-start(f32[5,64]{1,0:T(8,128)} %param.31) | copy-start | bytes 3844
  835.8 223.1 %copy-start.59 = (f32[64,739]{1,0:T(8,128)S(1)}, f32[64,739]{1,0:T(8,128)}, u32[]{:S(2)}) copy-start(f32[64,739]{1,0:T(8,128)} %param.26) | copy-start | bytes 567556
  835.8 223.1 %copy-start.69 = (f32[64,739]{1,0:T(8,128)S(1)}, f32[64,739]{1,0:T(8,128)}, u32[]{:S(2)}) copy-start(f32[64,739]{1,0:T(8,128)} %param.34) | copy-start | bytes 567556
  835.8 223.1 %copy-start.70 = (f32[64,739]{1,0:T(8,128)S(1)}, f32[64,739]{1,0:T(8,128)}, u32[]{:S(2)}) copy-start(f32[64,739]{1,0:T(8,128)} %param.30) | copy-start | bytes 567556
  835.9 224.9 %copy-start.31 = (f32[2,64,3072]{2,1,0:T(8,128)S(1)}, f32[2,64,3072]{2,1,0:T(8,128)}, u32[]{:S(2)}) copy-start(f32[2,64,3072]{2,1,0:T(8,128)} %param.25) | copy-start | bytes 4718596
  835.9 146.4 %reduce-scatter.19.cloned.1.call-start = ((), (), s32[]{:S(2)}) async-start(), calls=%async_computation.12 | async-start | bytes 294912
  839.3 194.9 %all-reduce.5.cloned.1.call-start = ((), (), s32[]{:S(2)}) async-start(), calls=%async_computation.15 | async-start | bytes 1769472 | tf_op jit(solution)/shard_map/psum | solution.py:327
  (103 other events, 1139.3 us)
Sparse Core Ops, SparseCore 0:
  10.2 69.4 all-gather.4
  89.7 51.2 all-gather.6
  227.0 53.3 all-gather.8
  544.1 53.9 reduce-scatter.12
  761.4 52.7 reduce-scatter.14
  816.3 31.8 reduce-scatter.20
  850.6 68.0 reduce-scatter.16
  921.4 29.0 reduce-scatter.22
  953.3 28.9 reduce-scatter.18
  985.3 48.8 all-reduce.4
where the time goes:
time: 1090 us; the launch traced here: 1070 us
  local copies, waits for them, and re-layouts  324 us (30%)
  waiting for transfers between devices  309 us (28%)
  other arithmetic  155 us (14%)
  matrix products  141 us (13%)
  blocking collectives  122 us (11%)
  between operations  22.8 us (2%)
    reshape x4, local copies, waits for them, and re-layouts, one_group(): jnp.stack([grad_key, grad_value], axis=2)  112 us
    unnamed x244, local copies, waits for them, and re-layouts  86.5 us
    scatter-add x2, other arithmetic, one_group(): carried = carried.at[indices.reshape(-1)].add(stacked)  71.9 us
    reduce_scatter x1, waiting for transfers between devices, local(): lax.psum_scatter(full_sums[1].astype(jnp.bfloat16), 'shd', scatter_dimens...  70.3 us
    unnamed x12, waiting for transfers between devices  61 us
    reduce_scatter x2, waiting for transfers between devices, local(): lax.psum_scatter(grad_pool.astype(jnp.bfloat16), 'grp', scatter_dimension...  56.7 us
    all_gather x2, waiting for transfers between devices, local(): source_pool = lax.all_gather(projected[:, D:], 'grp', axis=0, tiled=True)  46.9 us
    reshape x2, local copies, waits for them, and re-layouts, one_group(): pool_view[indices].reshape(group_size, SOURCES * BLOCK, 2, HEADS, HEAD_DIM)  44.1 us
  transfers between devices with their start and end apart: 10, of which 9 were waited for; matrix products, arithmetic and copies ran while one was open for 8% of the time, Pallas kernels for 0%

commit v1 on v0

v1 whole, which is shorter than its diff:
```python
import functools
import math

import jax
import jax.numpy as jnp
from jax import lax
from jax.experimental import pallas as pl
from jax.experimental.pallas import tpu as pltpu
from jax.sharding import PartitionSpec as P

D = 512
HEADS = 8
HEAD_DIM = 64
BLOCK = 128
SOURCES = 8
RATIO = 4
LAYERS = 2
CELL_BLOCK = RATIO * BLOCK
PICKED = SOURCES * BLOCK
LANES = 256
PACK = LANES // HEAD_DIM

eps_norm = 1e-05
score_scale = 0.125
clip_limit = 2.0
learn_rate = 0.02
decay_coef = 0.1
beta_one = 0.9
beta_two = 0.95
adam_eps = 1e-08

f32 = jnp.float32
bf16 = jnp.bfloat16
VMEM_LIMIT = 58 * 1024 * 1024


def nn(left, right):
    return jnp.dot(left, right, preferred_element_type=f32)


def tn(left, right):
    return lax.dot_general(left, right, (((0,), (0,)), ((), ())), preferred_element_type=f32)


def nt(left, right):
    return lax.dot_general(left, right, (((1,), (1,)), ((), ())), preferred_element_type=f32)


def norm_parts(values):
    average = jnp.mean(values, axis=-1, keepdims=True)
    centered = values - average
    variance = jnp.mean(centered * centered, axis=-1, keepdims=True)
    inverse = lax.rsqrt(variance + eps_norm)
    return (centered * inverse, inverse)


def norm_back(grad_out, normal, inverse, gain_row):
    grad_normal = grad_out * gain_row
    grad_gain = jnp.sum(grad_out * normal, axis=0, keepdims=True)
    mean_first = jnp.mean(grad_normal, axis=-1, keepdims=True)
    mean_second = jnp.mean(grad_normal * normal, axis=-1, keepdims=True)
    return (inverse * (grad_normal - mean_first - normal * mean_second), grad_gain)


def sigmoid(values):
    return 1.0 / (1.0 + jnp.exp(-values))


def node_match(node_row):
    rows = lax.broadcasted_iota(jnp.int32, (BLOCK, CELL_BLOCK), 0)
    return (rows == node_row).astype(f32)


def to_column(row):
    return jnp.transpose(jnp.broadcast_to(row, (BLOCK, row.shape[1])))[:, :1]


def spread_heads(rows):
    head = lax.broadcasted_iota(jnp.int32, rows.shape, 1) // HEAD_DIM
    zero = jnp.zeros_like(rows)
    return jnp.concatenate([jnp.where(head == h, rows, zero) for h in range(PACK)], axis=0)


def gather_heads(stacked):
    head = lax.broadcasted_iota(jnp.int32, (BLOCK, LANES), 1) // HEAD_DIM
    result = jnp.zeros((BLOCK, LANES), stacked.dtype)
    for h in range(PACK):
        result = jnp.where(head == h, stacked[h * BLOCK : (h + 1) * BLOCK], result)
    return result


def whole(memory_space=pltpu.VMEM):
    return pl.BlockSpec(memory_space=memory_space)


def call(body, out_shape, in_specs, scratch=(), flops=0, name=None, **kw):
    return pl.pallas_call(
        body,
        out_shape=out_shape,
        in_specs=in_specs,
        scratch_shapes=scratch,
        compiler_params=pltpu.CompilerParams(vmem_limit_bytes=VMEM_LIMIT),
        cost_estimate=pl.CostEstimate(flops=flops, bytes_accessed=8 << 20, transcendentals=0),
        name=name,
        **kw,
    )


def encode_body(cells_ref, node_ref, weight_ref, gain_ref, enc_ref, hidden_ref, normed_ref, count_ref):
    encoded = nn(cells_ref[...], weight_ref[...]).astype(bf16)
    enc_ref[...] = encoded
    match = node_match(node_ref[0])
    counts = jnp.sum(match, axis=1, keepdims=True)
    hidden = nn(match.astype(bf16), encoded) / counts
    hidden_ref[...] = hidden
    normal, _ = norm_parts(hidden)
    normed_ref[...] = (normal * gain_ref[0:1, :]).astype(bf16)
    count_ref[...] = jnp.broadcast_to(counts, (BLOCK, BLOCK))


def encode(cells, node, weight, gains):
    blocks = cells.shape[0] // CELL_BLOCK
    nodes = blocks * BLOCK
    row_spec = lambda rows, cols: pl.BlockSpec((rows, cols), lambda i: (i, 0))
    fixed = lambda a: pl.BlockSpec(a.shape, lambda i: (0,) * a.ndim)
    return pl.pallas_call(
        encode_body,
        grid=(blocks,),
        out_shape=(
            jax.ShapeDtypeStruct((cells.shape[0], D), bf16),
            jax.ShapeDtypeStruct((nodes, D), f32),
            jax.ShapeDtypeStruct((nodes, D), bf16),
            jax.ShapeDtypeStruct((nodes, BLOCK), f32),
        ),
        in_specs=[
            row_spec(CELL_BLOCK, cells.shape[1]),
            pl.BlockSpec((1, 1, CELL_BLOCK), lambda i: (i, 0, 0)),
            fixed(weight),
            fixed(gains),
        ],
        out_specs=(row_spec(CELL_BLOCK, D), row_spec(BLOCK, D), row_spec(BLOCK, D), row_spec(BLOCK, BLOCK)),
        compiler_params=pltpu.CompilerParams(vmem_limit_bytes=VMEM_LIMIT),
        cost_estimate=pl.CostEstimate(flops=10**9, bytes_accessed=6 << 20, transcendentals=0),
        name="encode",
    )(cells, node, weight, gains)


def layer_forward_body(
    layer, parts, adj_ref, own_ref, *refs
):
    part_refs = refs[:parts]
    h_ref, w_ref, gain_ref = refs[parts : parts + 3]
    next_ref, mid_ref, att_ref, normed_ref, q_ref, k_ref, v_ref, lse_ref = refs[parts + 3 : parts + 11]
    kg, vg = refs[parts + 11 :]
    start = 0
    for part in part_refs:
        rows = part.shape[0]
        for first in range(0, rows, 512):
            step = min(512, rows - first)
            block = part[first : first + step, :]
            k_ref[start : start + step, :] = nn(block, w_ref[:, D : 2 * D]).astype(bf16)
            v_ref[start : start + step, :] = nn(block, w_ref[:, 2 * D : 3 * D]).astype(bf16)
            start += step
    q_ref[...] = nn(own_ref[...], w_ref[:, :D]).astype(bf16)
    blocks = own_ref.shape[0] // BLOCK

    def one_block(r, _):
        rows = pl.ds(pl.multiple_of(r * BLOCK, BLOCK), BLOCK)
        for j in range(SOURCES):
            source = pl.ds(pl.multiple_of(adj_ref[r * SOURCES + j] * BLOCK, BLOCK), BLOCK)
            kg[j * BLOCK : (j + 1) * BLOCK, :] = k_ref[source, :]
            vg[j * BLOCK : (j + 1) * BLOCK, :] = v_ref[source, :]
        for g in range(D // LANES):
            lanes = slice(g * LANES, (g + 1) * LANES)
            query = spread_heads(q_ref[rows, lanes] * jnp.asarray(score_scale, bf16))
            scores = nt(query, kg[:, lanes])
            largest = jnp.max(scores, axis=-1, keepdims=True)
            exponent = jnp.exp(scores - largest)
            total = jnp.sum(exponent, axis=-1, keepdims=True)
            probs = (exponent * (1.0 / total)).astype(bf16)
            out = nn(probs, vg[:, lanes])
            att_ref[rows, lanes] = gather_heads(out).astype(bf16)
            log_sum = jnp.broadcast_to(largest + jnp.log(total), (PACK * BLOCK, BLOCK))
            lse_ref[r, g] = jnp.transpose(log_sum)[0:8, :]
        return 0

    lax.fori_loop(0, blocks, one_block, 0)
    middle = h_ref[...] + nn(att_ref[...], w_ref[:, 3 * D : 4 * D])
    mid_ref[...] = middle
    normal, _ = norm_parts(middle)
    normed = (normal * gain_ref[2 * layer + 1 : 2 * layer + 2, :]).astype(bf16)
    inner = nn(normed, w_ref[:, 4 * D : 5 * D])
    activated = (inner * sigmoid(inner)).astype(bf16)
    hidden = middle + nn(activated, w_ref[:, 5 * D :])
    next_ref[...] = hidden
    normal, _ = norm_parts(hidden)
    normed_ref[...] = (normal * gain_ref[2 * layer + 2 : 2 * layer + 3, :]).astype(bf16)


def layer_forward(layer, own, parts, adj, hidden, weights, gains):
    nodes = own.shape[0]
    blocks = nodes // BLOCK
    pool = sum(p.shape[0] for p in parts)
    sds = jax.ShapeDtypeStruct
    return call(
        functools.partial(layer_forward_body, layer, len(parts)),
        (
            sds((nodes, D), f32),
            sds((nodes, D), f32),
            sds((nodes, D), bf16),
            sds((nodes, D), bf16),
            sds((nodes, D), bf16),
            sds((pool, D), bf16),
            sds((pool, D), bf16),
            sds((blocks, D // LANES, 8, PACK * BLOCK), f32),
        ),
        [whole(pltpu.SMEM)] + [whole()] * (len(parts) + 4),
        scratch=(pltpu.VMEM((PICKED, D), bf16), pltpu.VMEM((PICKED, D), bf16)),
        flops=6 * 10**9,
        name=f"layer_forward_{layer}",
    )(adj, own, *parts, hidden, weights, gains)


def decode_body(
    inv_ref, enc_ref, node_ref, hidden_ref, area_ref, target_ref, w_ref, gain_ref,
    loss_ref, gcomb_ref, ghid_ref, gin_ref, gout_ref, ggain_ref,
):
    step = pl.program_id(0)
    match = node_match(node_ref[0]).astype(bf16)
    spread = tn(match, hidden_ref[...].astype(bf16))
    combined = enc_ref[...].astype(f32) + spread
    normal, inverse = norm_parts(combined)
    gain = gain_ref[2 * LAYERS : 2 * LAYERS + 1, :]
    normed = (normal * gain).astype(bf16)
    inner = nn(normed, w_ref[:, :D])
    sigma = sigmoid(inner)
    activated = (inner * sigma).astype(bf16)
    predicted = nn(activated, w_ref[:, D:])
    errors = predicted - target_ref[...].astype(f32)
    weighted = to_column(area_ref[0].astype(f32)) * errors
    part = jnp.sum(weighted * errors) * inv_ref[0]
    grad_pred = (2.0 * weighted * inv_ref[0]).astype(bf16)
    grad_out = tn(activated, grad_pred)
    grad_act = nt(grad_pred, w_ref[:, D:])
    grad_inner = (grad_act * (sigma * (1.0 + inner * (1.0 - sigma)))).astype(bf16)
    grad_in = tn(normed, grad_inner)
    grad_normed = nt(grad_inner, w_ref[:, :D])
    grad_comb, grad_gain = norm_back(grad_normed, normal, inverse, gain)
    grad_comb = grad_comb.astype(bf16)
    gcomb_ref[...] = grad_comb
    ghid_ref[...] = nn(match, grad_comb)

    @pl.when(step == 0)
    def _():
        loss_ref[0, 0] = part
        gin_ref[...] = grad_in
        gout_ref[...] = grad_out
        ggain_ref[...] = grad_gain

    @pl.when(step > 0)
    def _():
        loss_ref[0, 0] += part
        gin_ref[...] += grad_in
        gout_ref[...] += grad_out
        ggain_ref[...] += grad_gain


def decode(inv_area, encoded, node, hidden, areas, targets, weights, gains):
    blocks = encoded.shape[0] // CELL_BLOCK
    c_out = targets.shape[1]
    row_spec = lambda rows, cols: pl.BlockSpec((rows, cols), lambda i: (i, 0))
    fixed = lambda shape: pl.BlockSpec(shape, lambda i: (0,) * len(shape))
    line = pl.BlockSpec((1, 1, CELL_BLOCK), lambda i: (i, 0, 0))
    sds = jax.ShapeDtypeStruct
    return pl.pallas_call(
        decode_body,
        grid=(blocks,),
        out_shape=(
            sds((1, 1), f32),
            sds(encoded.shape, bf16),
            sds(hidden.shape, f32),
            sds((D, D), f32),
            sds((D, c_out), f32),
            sds((1, D), f32),
        ),
        in_specs=[
            whole(pltpu.SMEM),
            row_spec(CELL_BLOCK, D),
            line,
            row_spec(BLOCK, D),
            line,
            row_spec(CELL_BLOCK, c_out),
            fixed(weights.shape),
            fixed(gains.shape),
        ],
        out_specs=(
            pl.BlockSpec((1, 1), lambda i: (0, 0), memory_space=pltpu.SMEM),
            row_spec(CELL_BLOCK, D),
            row_spec(BLOCK, D),
            fixed((D, D)),
            fixed((D, c_out)),
            fixed((1, D)),
        ),
        compiler_params=pltpu.CompilerParams(vmem_limit_bytes=VMEM_LIMIT),
        cost_estimate=pl.CostEstimate(flops=5 * 10**9, bytes_accessed=8 << 20, transcendentals=0),
        name="decode",
    )(inv_area, encoded, node, hidden, areas, targets, weights, gains)


def first_norm_back(layer, gmid, grad_normed, hidden, gain_ref):
    normal, inverse = norm_parts(hidden)
    grad_first, grad_gain = norm_back(grad_normed, normal, inverse, gain_ref[2 * layer : 2 * layer + 1, :])
    return gmid + grad_first, grad_gain


def layer_backward_body(layer, above, adj_ref, *refs):
    refs = list(refs)
    take = lambda count: [refs.pop(0) for _ in range(count)]
    if above is None:
        (gh_ref,) = take(1)
    else:
        gmid_above, gown_above, habove_ref = take(3)
        received = take(above)
    mid_ref, att_ref, q_ref, k_ref, v_ref, lse_ref, w_ref, gain_ref = take(8)
    gmid_ref, gq_ref, gk_ref, gv_ref, gpool_ref, grest_ref, ggain_ref = take(7)
    if above is not None:
        (ggain_above_ref,) = take(1)
    kg, vg, gatt_ref, dk, dv = refs
    if above is None:
        grad_hidden = gh_ref[...]
    else:
        grad_normed = gown_above[...]
        for part in received:
            grad_normed = grad_normed + part[...].astype(f32)
        grad_hidden, ggain_above_ref[...] = first_norm_back(
            layer + 1, gmid_above[...], grad_normed, habove_ref[...], gain_ref
        )
    low = grad_hidden.astype(bf16)
    normal, inverse = norm_parts(mid_ref[...])
    gain = gain_ref[2 * layer + 1 : 2 * layer + 2, :]
    normed = (normal * gain).astype(bf16)
    inner = nn(normed, w_ref[:, 4 * D : 5 * D])
    sigma = sigmoid(inner)
    activated = (inner * sigma).astype(bf16)
    grest_ref[:, 2 * D :] = tn(activated, low).astype(bf16)
    grad_act = nt(low, w_ref[:, 5 * D :])
    grad_inner = (grad_act * (sigma * (1.0 + inner * (1.0 - sigma)))).astype(bf16)
    grest_ref[:, D : 2 * D] = tn(normed, grad_inner).astype(bf16)
    grad_normed = nt(grad_inner, w_ref[:, 4 * D : 5 * D])
    grad_mid, ggain_ref[...] = norm_back(grad_normed, normal, inverse, gain)
    grad_mid = grad_hidden + grad_mid
    gmid_ref[...] = grad_mid
    branch = grad_mid.astype(bf16)
    grest_ref[:, :D] = tn(att_ref[...], branch).astype(bf16)
    gatt_ref[...] = nt(branch, w_ref[:, 3 * D : 4 * D]).astype(bf16)
    dk[...] = jnp.zeros_like(dk)
    dv[...] = jnp.zeros_like(dv)
    blocks = mid_ref.shape[0] // BLOCK

    def one_block(r, _):
        rows = pl.ds(pl.multiple_of(r * BLOCK, BLOCK), BLOCK)
        sources = [
            pl.ds(pl.multiple_of(adj_ref[r * SOURCES + j] * BLOCK, BLOCK), BLOCK) for j in range(SOURCES)
        ]
        for j in range(SOURCES):
            kg[j * BLOCK : (j + 1) * BLOCK, :] = k_ref[sources[j], :]
            vg[j * BLOCK : (j + 1) * BLOCK, :] = v_ref[sources[j], :]
        for g in range(D // LANES):
            lanes = slice(g * LANES, (g + 1) * LANES)
            query = spread_heads(q_ref[rows, lanes] * jnp.asarray(score_scale, bf16))
            grad_out = spread_heads(gatt_ref[rows, lanes])
            probs = jnp.exp(nt(kg[:, lanes], query) - lse_ref[r, g, 0:1, :])
            grad_probs = nt(vg[:, lanes], grad_out)
            inner_sum = jnp.sum(probs * grad_probs, axis=0, keepdims=True)
            grad_scores = (probs * (grad_probs - inner_sum)).astype(bf16)
            grad_value = nn(probs.astype(bf16), grad_out)
            grad_key = nn(grad_scores, query)
            grad_query = gather_heads(tn(grad_scores, kg[:, lanes])) * score_scale
            gq_ref[rows, lanes] = grad_query.astype(bf16)
            for j in range(SOURCES):
                dk[sources[j], lanes] += grad_key[j * BLOCK : (j + 1) * BLOCK]
                dv[sources[j], lanes] += grad_value[j * BLOCK : (j + 1) * BLOCK]
        return 0

    lax.fori_loop(0, blocks, one_block, 0)
    for first in range(0, dk.shape[0], 512):
        rows = slice(first, first + 512)
        grad_key = dk[rows, :].astype(bf16)
        grad_value = dv[rows, :].astype(bf16)
        gk_ref[rows, :] = grad_key
        gv_ref[rows, :] = grad_value
        gpool_ref[rows, :] = (
            nt(grad_key, w_ref[:, D : 2 * D]) + nt(grad_value, w_ref[:, 2 * D : 3 * D])
        ).astype(bf16)


def layer_backward(layer, above, adj, mid, att, q, k, v, lse, weights, gains):
    nodes = mid.shape[0]
    pool = k.shape[0]
    sds = jax.ShapeDtypeStruct
    outs = [
        sds((nodes, D), f32),
        sds((nodes, D), bf16),
        sds((pool, D), bf16),
        sds((pool, D), bf16),
        sds((pool, D), bf16),
        sds((D, 3 * D), bf16),
        sds((1, D), f32),
    ]
    count = None if len(above) == 1 else len(above) - 3
    if count is not None:
        outs.append(sds((1, D), f32))
    return call(
        functools.partial(layer_backward_body, layer, count),
        tuple(outs),
        [whole(pltpu.SMEM)] + [whole()] * (len(above) + 8),
        scratch=(
            pltpu.VMEM((PICKED, D), bf16),
            pltpu.VMEM((PICKED, D), bf16),
            pltpu.VMEM((nodes, D), bf16),
            pltpu.VMEM((pool, D), f32),
            pltpu.VMEM((pool, D), f32),
        ),
        flops=12 * 10**9,
        name=f"layer_backward_{layer}",
    )(adj, *above, mid, att, q, k, v, lse, weights, gains)


def projection_back_body(parts, own_ref, *refs):
    part_refs = refs[:parts]
    gq_ref, gk_ref, gv_ref, w_ref, gown_ref, gw_ref = refs[parts:]
    gown_ref[...] = nt(gq_ref[...], w_ref[:, :D])
    gw_ref[:, :D] = tn(own_ref[...], gq_ref[...]).astype(bf16)
    for index, source in ((1, gk_ref), (2, gv_ref)):
        total = None
        start = 0
        for part in part_refs:
            rows = part.shape[0]
            value = tn(part[...], source[start : start + rows, :])
            total = value if total is None else total + value
            start += rows
        gw_ref[:, index * D : (index + 1) * D] = total.astype(bf16)


def projection_back(layer, own, parts, gq, gk, gv, weights):
    sds = jax.ShapeDtypeStruct
    return call(
        functools.partial(projection_back_body, len(parts)),
        (sds((own.shape[0], D), f32), sds((D, 3 * D), bf16)),
        [whole()] * (len(parts) + 5),
        flops=3 * 10**9,
        name=f"projection_back_{layer}",
    )(own, *parts, gq, gk, gv, weights)


def encode_back_body(parts, *refs):
    gmid_ref, gown_ref, h_ref = refs[:3]
    received = refs[3 : 3 + parts]
    gain_ref, cells_ref, node_ref, gcomb_ref, count_ref, gin_ref, ggain_ref = refs[3 + parts :]
    step = pl.program_id(0)
    grad_normed = gown_ref[...]
    for part in received:
        grad_normed = grad_normed + part[...].astype(f32)
    grad_hidden, grad_gain = first_norm_back(0, gmid_ref[...], grad_normed, h_ref[...], gain_ref)
    summed = (grad_hidden / count_ref[:, :1]).astype(bf16)
    match = node_match(node_ref[0]).astype(bf16)
    grad_enc = (gcomb_ref[...].astype(f32) + tn(match, summed)).astype(bf16)
    grad_in = tn(grad_enc, cells_ref[...])

    @pl.when(step == 0)
    def _():
        gin_ref[...] = grad_in
        ggain_ref[...] = grad_gain

    @pl.when(step > 0)
    def _():
        gin_ref[...] += grad_in
        ggain_ref[...] += grad_gain


def encode_back(gmid, gown, hidden, received, gains, cells, node, gcomb, counts):
    blocks = cells.shape[0] // CELL_BLOCK
    row_spec = lambda rows, cols: pl.BlockSpec((rows, cols), lambda i: (i, 0))
    fixed = lambda shape: pl.BlockSpec(shape, lambda i: (0,) * len(shape))
    node_spec = row_spec(BLOCK, D)
    sds = jax.ShapeDtypeStruct
    return pl.pallas_call(
        functools.partial(encode_back_body, len(received)),
        grid=(blocks,),
        out_shape=(sds((D, cells.shape[1]), f32), sds((1, D), f32)),
        in_specs=[node_spec] * (3 + len(received))
        + [
            fixed(gains.shape),
            row_spec(CELL_BLOCK, cells.shape[1]),
            pl.BlockSpec((1, 1, CELL_BLOCK), lambda i: (i, 0, 0)),
            row_spec(CELL_BLOCK, D),
            row_spec(BLOCK, BLOCK),
        ],
        out_specs=(fixed((D, cells.shape[1])), fixed((1, D))),
        compiler_params=pltpu.CompilerParams(vmem_limit_bytes=VMEM_LIMIT),
        cost_estimate=pl.CostEstimate(flops=10**9, bytes_accessed=8 << 20, transcendentals=0),
        name="encode_back",
    )(gmid, gown, hidden, *received, gains, cells, node, gcomb, counts)


def adam_step(gradient, weight, moment, square, factor, first_fix, second_fix, weight_decay):
    clipped = gradient * factor
    first = beta_one * moment + (1.0 - beta_one) * clipped
    second = beta_two * square + (1.0 - beta_two) * clipped * clipped
    delta = -learn_rate * (
        first / first_fix / (jnp.sqrt(second / second_fix) + adam_eps) + weight_decay * weight
    )
    return (delta, first, second)


def local(
    cells_in,
    targets,
    cell_areas,
    cell_node,
    adjacency,
    step_count,
    weight_in,
    weight_layer,
    weight_dec,
    norm_gains,
    moment_in,
    moment_layer,
    moment_dec,
    moment_gains,
    square_in,
    square_layer,
    square_dec,
    square_gains,
):
    blocks = adjacency.shape[0]
    areas_f = cell_areas.astype(f32)
    area_total = lax.psum(jnp.sum(areas_f), ("grp", "shd"))
    inv_area = (1.0 / area_total).reshape(1)
    low_in = lax.all_gather(weight_in.astype(bf16), "shd", axis=1, tiled=True)
    low_gains = lax.all_gather(norm_gains.astype(bf16), "shd", axis=1, tiled=True)
    low_layer = [
        lax.all_gather(weight_layer[i].astype(bf16), "shd", axis=0, tiled=True) for i in range(LAYERS)
    ]
    low_dec = lax.all_gather(weight_dec.astype(bf16), "shd", axis=0, tiled=True)
    gains = low_gains.astype(f32)
    node = cell_node.reshape(blocks, 1, CELL_BLOCK)
    areas = cell_areas.reshape(blocks, 1, CELL_BLOCK)
    adj = adjacency.reshape(-1)
    encoded, hidden, normed, counts = encode(cells_in, node, low_in, gains)
    kept = []
    for layer in range(LAYERS):
        pool = lax.all_gather(normed, "grp", axis=0, tiled=True)
        out = layer_forward(layer, normed, [pool], adj, hidden, low_layer[layer], gains)
        kept.append((hidden, normed, pool) + tuple(out[1:3]) + tuple(out[4:]))
        hidden, normed = out[0], out[3]
    loss_part, gcomb, ghid, gdec_in, gdec_out, gain_dec = decode(
        inv_area, encoded, node, hidden, areas, targets, low_dec, gains
    )
    gain_grads = [None] * (2 * LAYERS + 1)
    gain_grads[2 * LAYERS] = gain_dec
    layer_grads = [None] * LAYERS
    above = (ghid,)
    for layer in reversed(range(LAYERS)):
        h_in, normed, pool, mid, att, q, k, v, lse = kept[layer]
        back = layer_backward(layer, above, adj, mid, att, q, k, v, lse, low_layer[layer], gains)
        gmid, gq, gk, gv, gpool, grest, gain_grads[2 * layer + 1] = back[:7]
        if len(back) > 7:
            gain_grads[2 * layer + 2] = back[7]
        received = lax.psum_scatter(gpool, "grp", scatter_dimension=0, tiled=True)
        gown, gqkv = projection_back(layer, normed, [pool], gq, gk, gv, low_layer[layer])
        above = (gmid, gown, h_in, received)
        layer_grads[layer] = jnp.concatenate([gqkv, grest], axis=1)
    gmid, gown, h_in, received = above
    grad_in, gain_grads[0] = encode_back(gmid, gown, h_in, [received], gains, cells_in, node, gcomb, counts)
    grad_gains = jnp.concatenate(gain_grads, axis=0).T
    pieces = (
        grad_in.astype(bf16),
        layer_grads[0],
        layer_grads[1],
        jnp.concatenate([gdec_in, gdec_out], axis=1).astype(bf16),
        grad_gains.astype(bf16),
    )
    shards = [
        lax.psum(lax.psum_scatter(p, "shd", scatter_dimension=0, tiled=True), "grp").astype(f32) for p in pieces
    ]
    loss_group = lax.psum(loss_part[0, 0], "grp")
    group_sums = (shards[0].T, jnp.stack(shards[1:3], axis=0), shards[3], shards[4].T)
    squares_part = f32(0.0)
    for index_w in range(4):
        squares_part = squares_part + jnp.sum(group_sums[index_w] * group_sums[index_w])
    total_squares, loss_value = lax.psum((squares_part, loss_group), "shd")
    grad_norm = jnp.sqrt(total_squares)
    factor = clip_limit / jnp.maximum(grad_norm, clip_limit)
    step_value = step_count[0].astype(f32)
    first_fix = 1.0 - jnp.power(f32(beta_one), step_value)
    second_fix = 1.0 - jnp.power(f32(beta_two), step_value)
    weights = (weight_in, weight_layer, weight_dec, norm_gains)
    moments = (moment_in, moment_layer, moment_dec, moment_gains)
    squared = (square_in, square_layer, square_dec, square_gains)
    decays = (decay_coef, decay_coef, decay_coef, 0.0)
    deltas, firsts, seconds = ([], [], [])
    for index_w in range(4):
        delta, first, second = adam_step(
            group_sums[index_w],
            weights[index_w],
            moments[index_w],
            squared[index_w],
            factor,
            first_fix,
            second_fix,
            decays[index_w],
        )
        deltas.append(delta)
        firsts.append(first)
        seconds.append(second)
    return (loss_value, grad_norm, *deltas, *firsts, *seconds)


def solution(mesh):
    rows = P(("grp", "shd"), None)
    flat = P(("grp", "shd"))
    params = (P(None, "shd"), P(None, "shd", None), P("shd", None), P(None, "shd"))
    return jax.shard_map(
        local,
        mesh=mesh,
        in_specs=(rows, rows, flat, flat, rows, P()) + params * 3,
        out_specs=(P(), P()) + params * 3,
        check_vma=False,
    )
```

time: 1090 us -> 635 us (0.58)
  local copies, waits for them, and re-layouts: 324 us -> 9.9 us
  matrix products: 141 us -> 0 us
  Pallas kernels: 0 us -> 131 us
  other arithmetic: 155 us -> 25.5 us
    reshape x11 -> x1, local copies, waits for them, and re-layouts: 163 us -> 0.59 us  [local(): adj = adjacency.reshape(-1)]
    dot_general x48 -> x0, matrix products: 141 us -> none  [the longest x2 25.7 us: attend_backward(): jnp.einsum('gqhd,gkhd->ghqk', grad_out, value_grp, preferred_element_type...]
    pallas_call x0 -> x9, Pallas kernels: none -> 131 us  [the longest x2 51.6 us: layer_backward(): call(functools.partial(layer_backward_body, layer, count), tuple(outs), [...]
    unnamed x244 -> x54, local copies, waits for them, and re-layouts: 86.5 us -> 6.84 us
    scatter-add x2 -> x0, other arithmetic: 71.9 us -> none  [one_group(): carried = carried.at[indices.reshape(-1)].add(stacked)]
    reduce_scatter x4 -> x6, waiting for transfers between devices: 136 us -> 181 us  [the longest x4 138 us: local(): lax.psum_scatter(p, 'shd', scatter_dimension=0, tiled=True)]
    unnamed x12 -> x13, waiting for transfers between devices: 61 us -> 22.2 us
    convert_element_type x14 -> x4, other arithmetic: 36.6 us -> 2.7 us  [the longest x1 1.84 us: local(): grad_in.astype(bf16)]
  transfers between devices with their start and end apart: 10 -> 12, of which waited for: 9 -> 10; matrix products, arithmetic and copies ran while one was open for 8% -> 3% of each run, Pallas kernels for 0% -> 7%
where the time goes in v1:
time: 635 us; the launch traced here: 628 us
  waiting for transfers between devices  310 us (49%)
  Pallas kernels  131 us (21%)
  blocking collectives  129 us (20%)
  other arithmetic  25.5 us (4%)
  between operations  20.8 us (3%)
  local copies, waits for them, and re-layouts  9.9 us (2%)
    reduce_scatter x4, waiting for transfers between devices, local(): lax.psum_scatter(p, 'shd', scatter_dimension=0, tiled=True)  138 us
    pallas_call x2, Pallas kernels, layer_backward(): call(functools.partial(layer_backward_body, layer, count), tuple(outs), [...  51.6 us
    reduce_scatter x2, waiting for transfers between devices, local(): received = lax.psum_scatter(gpool, 'grp', scatter_dimension=0, tiled=True)  43.4 us
    all_gather x2, waiting for transfers between devices, local(): lax.all_gather(weight_layer[i].astype(bf16), 'shd', axis=0, tiled=True)  40.5 us
    psum x1, blocking collectives, local(): area_total = lax.psum(jnp.sum(areas_f), ('grp', 'shd'))  39.7 us
    pallas_call x2, Pallas kernels, layer_forward(): call(functools.partial(layer_forward_body, layer, len(parts)), (sds((node...  36.8 us
    psum x1, waiting for transfers between devices, local(): lax.psum(lax.psum_scatter(p, 'shd', scatter_dimension=0, tiled=True), 'grp')  33.8 us
    all_gather x2, waiting for transfers between devices, local(): pool = lax.all_gather(normed, 'grp', axis=0, tiled=True)  32.7 us
  transfers between devices with their start and end apart: 12, of which 10 were waited for; matrix products, arithmetic and copies ran while one was open for 3% of the time, Pallas kernels for 7%

profile of v1, /device:TPU:0, one launch (start us, length us, event | category | flops | bytes accessed | tf_op | source)
XLA Modules:
  0.0 627.6 jit_solution(18094861740762616896)
XLA Ops:
  8.0 14.5 %all-gather.2 = bf16[8,64,5]{1,2,0:T(8,128)(2,1)S(1)} all-gather(bf16[1,64,5]{1,2,0:T(8,128)(2,1)S(1)} %convert_bitcast_fusion), channel_id=1, replica_groups=mesh['grp'=4,'shd'=8] {'shd'}, dimensions={0}, use_global_device_ids=true | all-gather | bytes 5760 | tf_op jit(solution)/shard_map/all_gather | solution.py:541
  24.0 14.2 %all_gather.21 = bf16[227,512]{0,1:T(8,128)(2,1)S(1)} all-gather(bf16[227,64]{0,1:T(8,128)(2,1)S(1)} %convert_element_type.47), channel_id=1, replica_groups=mesh['grp'=4,'shd'=8] {'shd'}, dimensions={1}, use_global_device_ids=true | all-gather | bytes 261504 | tf_op jit(solution)/shard_map/all_gather | solution.py:540
  47.7 32.7 %all-gather.8.cloned.1.call-done.refs_0_ = bf16[2048,512]{1,0:T(8,128)(2,1)} async-done(((bf16[512,512]{1,0:T(8,128)(2,1)}), bf16[2048,512]{1,0:T(8,128)(2,1)}) %all-gather.8.cloned.1.call-update) | async-done | bytes 2097168 | tf_op jit(solution)/shard_map/all_gather | solution.py:553
  80.4 40.5 %all-gather.12.cloned.1.call-done = bf16[1,512,3072]{2,1,0:T(8,128)(2,1)} async-done(((bf16[1,64,3072]{2,1,0:T(8,128)(2,1)}), bf16[1,512,3072]{2,1,0:T(8,128)(2,1)}) %all-gather.12.cloned.1.call-update) | async-done | bytes 3145744 | tf_op jit(solution)/shard_map/all_gather | solution.py:543
  120.8 18.4 %layer_forward_0.1 = (f32[512,512]{1,0:T(8,128)}, f32[512,512]{1,0:T(8,128)}, bf16[512,512]{1,0:T(8,128)(2,1)}, bf16[512,512]{1,0:T(8,128)(2,1)}, bf16[512,512]{...) custom-call(s32[32]{0:T(128)} %reshape.53.adj_ref, ...), custom_call_target="tpu_custom_call" | custom-call | flops 6000000000 | bytes 8388608 | tf_op jit(solution)/shard_map/layer_forward_0/pallas_call | solution.py:205
  140.0 39.7 %psum.63 = f32[]{:T(128)} all-reduce(f32[]{:T(128)} %convert_reduce_fusion), channel_id=1, replica_groups=mesh['grp'=4,'shd'=8] {'grp','shd'}, use_global_device_ids=true, to_apply=%region_1.0 | all-reduce | flops 1 | bytes 8 | tf_op jit(solution)/shard_map/psum | solution.py:538
  181.7 16.5 %all_gather.27.w_ref = bf16[512,739]{1,0:T(8,128)(2,1)} all-gather(bf16[64,739]{1,0:T(8,128)(2,1)S(1)} %convert_element_type.52), channel_id=1, replica_groups=mesh['grp'=4,'shd'=8] {'shd'}, dimensions={0}, use_global_device_ids=true | all-gather | bytes 851328 | tf_op jit(solution)/shard_map/all_gather | solution.py:545
  198.1 18.4 %layer_forward_1.1 = (f32[512,512]{1,0:T(8,128)}, f32[512,512]{1,0:T(8,128)}, bf16[512,512]{1,0:T(8,128)(2,1)}, bf16[512,512]{1,0:T(8,128)(2,1)}, bf16[512,512]{...) custom-call(s32[32]{0:T(128)} %reshape.53.adj_ref, ...), custom_call_target="tpu_custom_call" | custom-call | flops 6000000000 | bytes 8388608 | tf_op jit(solution)/shard_map/layer_forward_1/pallas_call | solution.py:205
  216.5 15.0 %decode.1 = (f32[1,1]{1,0:T(1,128)}, bf16[2048,512]{1,0:T(8,128)(2,1)}, f32[512,512]{1,0:T(8,128)}, f32[512,512]{1,0:T(8,128)}, f32[512,227]{1,0:T(8,128)}, /*index=5*/f32[1,512]{1,0:T(1,128)}) custom-call(f32[1]{0:T(128)} %bitcast.1.inv_ref, bf16[2048,512]{1,0:T(8,128)(2,1)} %get-tuple-element.60.enc_ref, s32[4,1,512]{2,1,0:T(1,128)} %bitcast.55, ...), custom_call_target="tpu_custom_call" | custom-call | flops 5000000000 | bytes 8388608 | tf_op jit(solution)/shard_map/decode/pallas_call | solution.py:275
  231.5 25.1 %layer_backward_1.1 = (f32[512,512]{1,0:T(8,128)}, bf16[512,512]{1,0:T(8,128)(2,1)}, bf16[2048,512]{1,0:T(8,128)(2,1)}, bf16[2048,512]{1,0:T(8,128)(2,1)}, bf16[...) custom-call(s32[32]{0:T(128)} %reshape.53.adj_ref, f32[512,512]{1,0:T(8,128)} %get-tuple-element.67.refs_0_, ...), custom_call_target="tpu_custom_call" | custom-call | flops 12000000000 | bytes 8388608 | tf_op jit(solution)/shard_map/layer_backward_1/pallas_call | solution.py:413
  256.7 8.1 %projection_back_1.1 = (f32[512,512]{1,0:T(8,128)}, bf16[512,1536]{1,0:T(8,128)(2,1)}) custom-call(bf16[512,512]{1,0:T(8,128)(2,1)} %get-tuple-element.63.own_ref, bf16[2048,512]{1,0:T(8,128)(2,1)} %all-gather.10.cloned.1.call-done.refs_0_, bf16[512,512]{1,0:T(8,128)(2,1)} %get-tuple-element.75.refs_1_, bf16[2048,512]{1,0:T(8,128)(2,1)} %get-tuple-element.76.refs_2_, ...), custom_call_target="tpu_custom_call" | custom-call | flops 3000000000 | bytes 8388608 | tf_op jit(solution)/shard_map/projection_back_1/pallas_call | solution.py:447
  264.8 27.3 %reduce-scatter.10.cloned.1.call-done.refs_3_ = bf16[512,512]{1,0:T(8,128)(2,1)} async-done(((bf16[2048,512]{1,0:T(8,128)(2,1)}), bf16[512,512]{1,0:T(8,128)(2,1)}) %reduce-scatter.10.cloned.1.call-update) | async-done | bytes 524304 | tf_op jit(solution)/shard_map/reduce_scatter | solution.py:570
  292.1 26.6 %layer_backward_0.1 = (f32[512,512]{1,0:T(8,128)}, bf16[512,512]{1,0:T(8,128)(2,1)}, bf16[2048,512]{1,0:T(8,128)(2,1)}, bf16[2048,512]{1,0:T(8,128)(2,1)}, bf16[...) custom-call(s32[32]{0:T(128)} %reshape.53.adj_ref, ...), custom_call_target="tpu_custom_call" | custom-call | flops 12000000000 | bytes 8388608 | tf_op jit(solution)/shard_map/layer_backward_0/pallas_call | solution.py:413
  325.5 8.2 %projection_back_0.1 = (f32[512,512]{1,0:T(8,128)}, bf16[512,1536]{1,0:T(8,128)(2,1)}) custom-call(bf16[512,512]{1,0:T(8,128)(2,1)} %get-tuple-element.61.own_ref, bf16[2048,512]{1,0:T(8,128)(2,1)} %all-gather.8.cloned.1.call-done.refs_0_, bf16[512,512]{1,0:T(8,128)(2,1)} %get-tuple-element.87.refs_1_, bf16[2048,512]{1,0:T(8,128)(2,1)} %get-tuple-element.88.refs_2_, ...), custom_call_target="tpu_custom_call" | custom-call | flops 3000000000 | bytes 8388608 | tf_op jit(solution)/shard_map/projection_back_0/pallas_call | solution.py:447
  338.0 16.0 %reduce-scatter.12.cloned.1.call-done.refs_3_ = bf16[512,512]{1,0:T(8,128)(2,1)} async-done(((bf16[2048,512]{1,0:T(8,128)(2,1)}), bf16[512,512]{1,0:T(8,128)(2,1)}) %reduce-scatter.12.cloned.1.call-update) | async-done | bytes 524304 | tf_op jit(solution)/shard_map/reduce_scatter | solution.py:570
  364.3 24.1 %reduce-scatter.20.cloned.1.call-done = bf16[64,739]{1,0:T(8,128)(2,1)} async-done(((bf16[512,739]{1,0:T(8,128)(2,1)}), bf16[64,739]{1,0:T(8,128)(2,1)}) %reduce-scatter.20.cloned.1.call-update) | async-done | bytes 94608 | tf_op jit(solution)/shard_map/reduce_scatter | solution.py:585
  388.4 40.9 %reduce-scatter.18.cloned.1.call-done = bf16[64,3072]{1,0:T(8,128)(2,1)} async-done(((bf16[512,3072]{1,0:T(8,128)(2,1)}), bf16[64,3072]{1,0:T(8,128)(2,1)}) %reduce-scatter.18.cloned.1.call-update) | async-done | bytes 393232 | tf_op jit(solution)/shard_map/reduce_scatter | solution.py:585
  429.3 41.9 %reduce-scatter.16.cloned.1.call-done = bf16[64,3072]{1,0:T(8,128)(2,1)} async-done(((bf16[512,3072]{1,0:T(8,128)(2,1)}), bf16[64,3072]{1,0:T(8,128)(2,1)}) %reduce-scatter.16.cloned.1.call-update) | async-done | bytes 393232 | tf_op jit(solution)/shard_map/reduce_scatter | solution.py:585
  471.9 10.5 %psum.64 = f32[]{:T(128)} all-reduce(f32[]{:T(128)} %bitcast.9), channel_id=1, replica_groups=mesh['grp'=4,'shd'=8] {'grp'}, use_global_device_ids=true, to_apply=%region_2.0 | all-reduce | flops 1 | bytes 8 | tf_op jit(solution)/shard_map/psum | solution.py:587
  482.4 21.4 %reduce-scatter.22.cloned.1.call-done = bf16[64,5]{1,0:T(8,128)(2,1)} async-done(((bf16[512,5]{1,0:T(8,128)(2,1)}), bf16[64,5]{1,0:T(8,128)(2,1)}) %reduce-scatter.22.cloned.1.call-update) | async-done | bytes 656
  504.5 31.0 %reduce-scatter.14.cloned.1.call-done = bf16[64,227]{1,0:T(8,128)(2,1)} async-done(((bf16[512,227]{1,0:T(8,128)(2,1)}), bf16[64,227]{1,0:T(8,128)(2,1)}) %reduce-scatter.14.cloned.1.call-update) | async-done | bytes 29072 | tf_op jit(solution)/shard_map/reduce_scatter | solution.py:585
  535.6 17.2 %all-reduce.1 = (bf16[64,227]{1,0:T(8,128)(2,1)S(1)}, bf16[64,5]{0,1:T(8,128)(2,1)S(1)}) all-reduce(bf16[64,227]{1,0:T(8,128)(2,1)} %reduce-scatter.14.cloned.1.call-done, bf16[64,5]{0,1:T(8,128)(2,1)S(1)} %copy.48), channel_id=1, replica_groups=mesh['grp'=4,'shd'=8] {'grp'}, use_global_device_ids=true, to_apply=%region_7.0 | all-reduce | flops 14848 | bytes 59392 | tf_op jit(solution)/shard_map/psum | solution.py:585
  554.0 33.8 %all-reduce.5.cloned.1.call-done = (bf16[1,64,3072]{2,1,0:T(8,128)(2,1)}, bf16[1,64,3072]{2,1,0:T(8,128)(2,1)}, bf16[64,739]{1,0:T(8,128)(2,1)}) async-done(((bf16[1,64,3072]{2,1,0:T(8,128)(2,1)}, bf16[1,64,3072]{2,1,0:T(8,128)(2,1)}, bf16[64,739]{1,0:T(8,128)(2,1)}), (bf16[1,64,3072]{2,1,0:T(8,128)(2,1)}, bf16[1,64,3072]{2,1,0:T(8,128)(2,1)}, bf16[64,739]{1,0:T(8,128)(2,1)})) %all-reduce.5.cloned.1.call-update) | async-done | bytes 881040 | tf_op jit(solution)/shard_map/psum | solution.py:585
  594.1 16.8 %all-reduce = (f32[]{:T(128)}, f32[]{:T(128)}) all-reduce(f32[]{:T(128)} %psum.64, f32[]{:T(128)S(6)} %add.103), channel_id=1, replica_groups=mesh['grp'=4,'shd'=8] {'shd'}, use_global_device_ids=true, to_apply=%region_3.0 | all-reduce | flops 2 | bytes 16 | tf_op jit(solution)/shard_map/psum | solution.py:592
  (112 shorter events, 48.2 us)
Async XLA Ops:
  7.2 31.8 %copy-start.7 = (bf16[2048,227]{0,1:T(8,128)(2,1)S(1)}, bf16[2048,227]{0,1:T(8,128)(2,1)}, u32[]{:S(2)}) copy-start(bf16[2048,227]{0,1:T(8,128)(2,1)} %param.18) | copy-start | bytes 2789380
  7.2 73.2 %all-gather.8.cloned.1.call-start = ((), (), s32[]{:S(2)}) async-start(), calls=%async_computation.7 | async-start | bytes 2621440 | tf_op jit(solution)/shard_map/all_gather | solution.py:553
  45.1 75.7 %all-gather.12.cloned.1.call-start = ((), (), s32[]{:S(2)}) async-start(), calls=%async_computation.15 | async-start | bytes 3538944 | tf_op jit(solution)/shard_map/all_gather | solution.py:543
  46.3 151.9 %all-gather.14.cloned.1.call-start = ((), (), s32[]{:S(2)}) async-start(), calls=%async_computation.16 | async-start | bytes 3538944 | tf_op jit(solution)/shard_map/all_gather | solution.py:543
  47.0 151.1 %all-gather.10.cloned.1.call-start = ((), (), s32[]{:S(2)}) async-start(), calls=%async_computation.8 | async-start | bytes 2621440 | tf_op jit(solution)/shard_map/all_gather | solution.py:553
  120.8 58.8 %copy-start.9 = (f32[64,739]{1,0:T(8,128)S(1)}, f32[64,739]{1,0:T(8,128)}, u32[]{:S(2)}) copy-start(f32[64,739]{1,0:T(8,128)} %param.26) | copy-start | bytes 567556
  120.8 58.8 %copy-start.8 = (bf16[2048,227]{0,1:T(8,128)(2,1)S(1)}, bf16[2048,227]{0,1:T(8,128)(2,1)}, u32[]{:S(2)}) copy-start(bf16[2048,227]{0,1:T(8,128)(2,1)} %param.19) | copy-start | bytes 2789380
  139.3 152.8 %reduce-scatter.10.cloned.1.call-start = ((), (), s32[]{:S(2)}) async-start(), calls=%async_computation.9 | async-start | bytes 2621440 | tf_op jit(solution)/shard_map/reduce_scatter | solution.py:570
  256.6 97.4 %reduce-scatter.12.cloned.1.call-start = ((), (), s32[]{:S(2)}) async-start(), calls=%async_computation.10 | async-start | bytes 2621440 | tf_op jit(solution)/shard_map/reduce_scatter | solution.py:570
  318.7 69.7 %reduce-scatter.20.cloned.1.call-start = ((), (), s32[]{:S(2)}) async-start(), calls=%async_computation.14 | async-start | bytes 884736 | tf_op jit(solution)/shard_map/reduce_scatter | solution.py:585
  321.2 108.1 %reduce-scatter.18.cloned.1.call-start = ((), (), s32[]{:S(2)}) async-start(), calls=%async_computation.13 | async-start | bytes 3538944 | tf_op jit(solution)/shard_map/reduce_scatter | solution.py:585
  325.4 145.8 %reduce-scatter.16.cloned.1.call-start = ((), (), s32[]{:S(2)}) async-start(), calls=%async_computation.12 | async-start | bytes 3538944 | tf_op jit(solution)/shard_map/reduce_scatter | solution.py:585
  337.3 166.4 %reduce-scatter.22.cloned.1.call-start = ((), (), s32[]{:S(2)}) async-start(), calls=%async_computation.17 | async-start | bytes 147456
  362.2 249.4 %copy-start.16 = (f32[5,64]{1,0:T(8,128)S(1)}, f32[5,64]{1,0:T(8,128)}, u32[]{:S(2)}) copy-start(f32[5,64]{1,0:T(8,128)} %param.27) | copy-start | bytes 3844
  362.2 249.4 %copy-start.18 = (f32[5,64]{1,0:T(8,128)S(1)}, f32[5,64]{1,0:T(8,128)}, u32[]{:S(2)}) copy-start(f32[5,64]{1,0:T(8,128)} %param.35) | copy-start | bytes 3844
  362.2 249.4 %copy-start.19 = (f32[5,64]{1,0:T(8,128)S(1)}, f32[5,64]{1,0:T(8,128)}, u32[]{:S(2)}) copy-start(f32[5,64]{1,0:T(8,128)} %param.31) | copy-start | bytes 3844
  362.2 250.1 %copy-start.11 = (f32[227,64]{0,1:T(8,128)S(1)}, f32[227,64]{0,1:T(8,128)}, u32[]{:S(2)}) copy-start(f32[227,64]{0,1:T(8,128)} %param.24) | copy-start | bytes 174340
  362.2 250.0 %copy-start.14 = (f32[227,64]{0,1:T(8,128)S(1)}, f32[227,64]{0,1:T(8,128)}, u32[]{:S(2)}) copy-start(f32[227,64]{0,1:T(8,128)} %param.32) | copy-start | bytes 174340
  362.3 250.0 %copy-start.15 = (f32[227,64]{0,1:T(8,128)S(1)}, f32[227,64]{0,1:T(8,128)}, u32[]{:S(2)}) copy-start(f32[227,64]{0,1:T(8,128)} %param.28) | copy-start | bytes 174340
  362.3 173.3 %reduce-scatter.14.cloned.1.call-start = ((), (), s32[]{:S(2)}) async-start(), calls=%async_computation.11 | async-start | bytes 294912 | tf_op jit(solution)/shard_map/reduce_scatter | solution.py:585
  362.3 250.7 %copy-start.12 = (f32[64,739]{1,0:T(8,128)S(1)}, f32[64,739]{1,0:T(8,128)}, u32[]{:S(2)}) copy-start(f32[64,739]{1,0:T(8,128)} %param.34) | copy-start | bytes 567556
  362.4 250.7 %copy-start.13 = (f32[64,739]{1,0:T(8,128)S(1)}, f32[64,739]{1,0:T(8,128)}, u32[]{:S(2)}) copy-start(f32[64,739]{1,0:T(8,128)} %param.30) | copy-start | bytes 567556
  364.2 223.5 %all-reduce.5.cloned.1.call-start = ((), (), s32[]{:S(2)}) async-start(), calls=%async_computation.18 | async-start | bytes 1769472 | tf_op jit(solution)/shard_map/psum | solution.py:585
  587.7 27.1 %copy-start.2 = (bf16[1,64,3072]{2,1,0:T(8,128)(2,1)S(1)}, bf16[1,64,3072]{2,1,0:T(8,128)(2,1)}, u32[]{:S(2)}) copy-start(bf16[1,64,3072]{2,1,0:T(8,128)(2,1)} %get-tuple-element.111) | copy-start | bytes 1179652
  (13 other events, 70.6 us)
Sparse Core Ops, SparseCore 0:
  45.3 35.0 all-gather.7
  82.6 38.2 all-gather.11
  123.0 37.2 all-gather.13
  162.1 34.7 all-gather.9
  256.7 35.3 reduce-scatter.9
  318.8 35.1 reduce-scatter.11
  356.3 32.0 reduce-scatter.19
  390.7 38.5 reduce-scatter.17
  431.6 39.5 reduce-scatter.15
  473.8 29.8 reduce-scatter.21
  506.6 28.9 reduce-scatter.13
  538.8 48.8 all-reduce.4
